TPU v7x, 256 devices: a whole 4x4x8 slice. The times are simulated.
256 devices in a mesh: row: 8 (over z_hi, x), col: 32 (over z_lo, y, core).
Axes of the slice: x: 4, y: 4, z: 8 (z_hi: 2, z_lo: 4; z = z_hi * 4 + z_lo), core: 2. Of those that a mesh axis runs over, the one named last changes fastest.
Arguments:
- contexts: bfloat16 [32768, 128], P(('row', 'col')), may hold values from -8 to 8
- logged_actions: int32 [32768], P(('row', 'col')), may hold values from 0 to 131041
- policy_actions: int32 [32768, 8], P(('row', 'col')), may hold values from 0 to 131041
- rewards: float32 [32768], P(('row', 'col')), may hold values from 0.2 to 2
Outputs:
- weights: float32 [32768, 8], P(('row', 'col'))
- residual: float32 [32768, 8], P(('row', 'col'))
- values: float32 [8], replicated
All inputs are finite; a program needn't handle non-finite values.
Results may differ from a plain program's by a relative error of at most 0.0056.
Values may be sent and summed in bfloat16 or wider, within the bound.
No kernel may reach another device: no remote copies, remote signals or barrier semaphores. Data moves between devices by JAX's collectives and lax.ppermute only.
A program may use at most 64 MiB of HBM per device.

v0:
```python
import math
import jax
import jax.numpy as jnp
from jax import lax
from jax.sharding import PartitionSpec as P

NPOL = 8
NACT = 16
CATALOG = 131042
ridge = 0.1
group_size = 16
stride_base = 1009
phase_step = 0.37
two_pi = 2.0 * math.pi


def action_features(chosen, width):
    levels = jnp.arange(width, dtype=jnp.int32)
    multipliers = 1 + stride_base * levels
    turned = chosen[..., None] * multipliers % CATALOG
    angles = turned.astype(jnp.float32) * (two_pi / CATALOG) + phase_step * levels.astype(
        jnp.float32
    )
    wave_terms = math.sqrt(2.0 / width) * jnp.cos(angles)
    constant_term = jnp.full(wave_terms.shape, 1.0 / math.sqrt(width), jnp.float32)
    return jnp.where(levels == 0, constant_term, wave_terms).astype(jnp.bfloat16)


def select_actions(products, onehot):
    shaped = products.reshape(
        products.shape[:-1] + (products.shape[-1] // onehot.shape[-1], onehot.shape[-1])
    )
    return jnp.sum(shaped * jnp.expand_dims(onehot.astype(jnp.float32), -2), axis=-1)


def kernel_tiles(left_tiles, right_tiles, left_squares, right_squares):
    inner = jnp.einsum("grd,gsd->grs", left_tiles, right_tiles, preferred_element_type=jnp.float32)
    expo = (2.0 * inner - left_squares[:, :, None] - right_squares[:, None, :]) / left_tiles.shape[
        -1
    ]
    return jnp.exp(expo).astype(jnp.bfloat16)


def tile_terms(kernel, left_matrix, right_matrix, left_onehot, right_onehot):
    toward_left = jnp.einsum(
        "grs,gsm->grm", kernel, right_matrix, preferred_element_type=jnp.float32
    )
    toward_right = jnp.einsum(
        "grs,grm->gsm", kernel, left_matrix, preferred_element_type=jnp.float32
    )
    return (select_actions(toward_left, left_onehot), select_actions(toward_right, right_onehot))


def listed_pass(
    left_ctx,
    left_squares,
    left_matrix,
    left_onehot,
    right_ctx,
    right_squares,
    right_matrix,
    right_onehot,
    placed,
    diagonal,
):
    left_count = left_ctx.shape[0]
    tile_rows = left_ctx.shape[1]
    right_count = right_ctx.shape[0]
    policies = left_matrix.shape[-1] // left_onehot.shape[-1]
    flat_placed = placed.reshape(-1)
    flat_diagonal = diagonal.reshape(-1)
    plan = jnp.argsort(1 - flat_placed, stable=True)
    active_count = jnp.sum(flat_placed)
    rounds = (active_count + group_size - 1) // group_size

    def advance(round_index, carried):
        row_sums, column_sums = carried
        picked = lax.dynamic_slice_in_dim(plan, round_index * group_size, group_size)
        left_pick = picked // right_count
        right_pick = picked % right_count
        live_flags = jnp.take(flat_placed, picked).astype(jnp.float32)
        mirror_flags = live_flags * (1 - jnp.take(flat_diagonal, picked)).astype(jnp.float32)
        kernel = kernel_tiles(
            left_ctx[left_pick],
            right_ctx[right_pick],
            left_squares[left_pick],
            right_squares[right_pick],
        )
        toward_left, toward_right = tile_terms(
            kernel,
            left_matrix[left_pick],
            right_matrix[right_pick],
            left_onehot[left_pick],
            right_onehot[right_pick],
        )
        row_sums = row_sums.at[left_pick].add(toward_left * live_flags[:, None, None])
        column_sums = column_sums.at[right_pick].add(toward_right * mirror_flags[:, None, None])
        return (row_sums, column_sums)

    start_rows = jnp.zeros((left_count, tile_rows, policies), jnp.float32)
    start_columns = jnp.zeros((right_count, tile_rows, policies), jnp.float32)
    return lax.fori_loop(0, rounds, advance, (start_rows, start_columns))


def on_device(contexts, logged_actions, policy_actions, rewards):
    tile_rows, feature_count = contexts.shape
    left_count = lax.axis_size("col")
    right_count = lax.axis_size("row")
    factor = NACT / (tile_rows * left_count * right_count)
    own_column = lax.axis_index("col")
    own_row = lax.axis_index("row")
    left_ids = jnp.arange(left_count, dtype=jnp.int32)[:, None]
    right_ids = jnp.arange(right_count, dtype=jnp.int32)[None, :]
    first_owner = own_row * left_count + left_ids
    second_owner = right_ids * left_count + own_column
    parity = (first_owner + second_owner) % 2
    placed = jnp.where(
        first_owner == second_owner, 1, jnp.where(first_owner < second_owner, parity, 1 - parity)
    )
    diagonal = ((left_ids == own_column) & (right_ids == own_row)).astype(jnp.int32)
    left_logged, left_policy = (
        lax.all_gather(logged_actions, "col", axis=0, tiled=True),
        lax.all_gather(policy_actions, "col", axis=0, tiled=True),
    )
    right_logged, right_policy = (
        lax.all_gather(logged_actions, "row", axis=0, tiled=True),
        lax.all_gather(policy_actions, "row", axis=0, tiled=True),
    )
    left_onehot = action_features(left_logged, NACT).reshape(left_count, tile_rows, NACT)
    right_onehot = action_features(right_logged, NACT).reshape(right_count, tile_rows, NACT)
    left_first = action_features(left_policy, NACT).reshape(left_count, tile_rows, NPOL * NACT)
    right_first = action_features(right_policy, NACT).reshape(right_count, tile_rows, NPOL * NACT)
    right_ctx = lax.all_gather(contexts, "row", axis=0, tiled=True).reshape(
        right_count, tile_rows, feature_count
    )
    right_squares = jnp.sum(right_ctx.astype(jnp.float32) ** 2, axis=2)
    left_ctx = lax.all_gather(contexts, "col", axis=0, tiled=True).reshape(
        left_count, tile_rows, feature_count
    )
    left_squares = jnp.sum(left_ctx.astype(jnp.float32) ** 2, axis=2)

    def sweep(left_matrix, right_matrix):
        return listed_pass(
            left_ctx,
            left_squares,
            left_matrix,
            left_onehot,
            right_ctx,
            right_squares,
            right_matrix,
            right_onehot,
            placed,
            diagonal,
        )

    def reduce_terms(toward_left, toward_right):
        mine_left = lax.psum_scatter(toward_left, "col", scatter_dimension=0, tiled=True)
        mine_right = lax.psum_scatter(toward_right, "row", scatter_dimension=0, tiled=True)
        return factor * (mine_left[0] + mine_right[0])

    first_left, first_right = sweep(left_first, right_first)
    right_side = reduce_terms(first_left, first_right)
    right_low = right_side.astype(jnp.bfloat16)
    left_rhs = lax.all_gather(right_low, "col", axis=0, tiled=True).reshape(
        left_count, tile_rows, NPOL
    )
    right_rhs = lax.all_gather(right_low, "row", axis=0, tiled=True).reshape(
        right_count, tile_rows, NPOL
    )
    left_second = (left_onehot[:, :, None, :] * left_rhs[:, :, :, None]).reshape(
        left_count, tile_rows, NPOL * NACT
    )
    right_second = (right_onehot[:, :, None, :] * right_rhs[:, :, :, None]).reshape(
        right_count, tile_rows, NPOL * NACT
    )
    second_left, second_right = sweep(left_second, right_second)
    image = reduce_terms(second_left, second_right) + ridge * right_side
    norm_sums, curvature, reward_sums = lax.psum(
        (
            jnp.sum(right_side * right_side, axis=0),
            jnp.sum(right_side * image, axis=0),
            jnp.sum(rewards[:, None] * right_side, axis=0),
        ),
        ("row", "col"),
    )
    alpha = norm_sums / curvature
    weights = alpha[None, :] * right_side
    residual = right_side - alpha[None, :] * image
    values = alpha * reward_sums / (tile_rows * left_count * right_count)
    return (weights, residual, values)


def solution(mesh):
    placed = (
        P(("row", "col"), None),
        P(("row", "col")),
        P(("row", "col"), None),
        P(("row", "col")),
    )
    return jax.shard_map(
        on_device,
        mesh=mesh,
        in_specs=placed,
        out_specs=(P(("row", "col"), None), P(("row", "col"), None), P()),
        check_vma=False,
    )
```

profile of v0, /device:TPU:1, one launch (start us, length us, event | category | flops | bytes accessed | tf_op | source)
XLA Modules:
  0.0 1289.7 jit_solution(7908967299347687956)
XLA Ops:
  11.6 3.2 sort.19
  14.8 29.4 %all-gather.1 = s32[8,1,128]{2,1,0:T(1,128)S(1)} all-gather(s32[1,1,128]{2,1,0:T(1,128)} %bitcast.113), channel_id=1, replica_groups=mesh['row'=8,'col'=32] {'row'}, dimensions={0}, use_global_device_ids=true | all-gather | bytes 4608 | tf_op jit(solution)/shard_map/all_gather | solution.py:126
  44.2 46.1 %all-gather = s32[32,1,128]{2,1,0:T(1,128)S(1)} all-gather(s32[1,1,128]{2,1,0:T(1,128)} %bitcast.114), channel_id=1, replica_groups=mesh['row'=8,'col'=32] {'col'}, dimensions={0}, use_global_device_ids=true | all-gather | bytes 16896 | tf_op jit(solution)/shard_map/all_gather | solution.py:122
  90.3 37.4 %all_gather.26 = s32[1024,8]{0,1:T(8,128)S(1)} all-gather(s32[128,8]{0,1:T(8,128)} %param.12), channel_id=1, replica_groups=mesh['row'=8,'col'=32] {'row'}, dimensions={0}, use_global_device_ids=true | all-gather | bytes 36864 | tf_op jit(solution)/shard_map/all_gather | solution.py:127
  127.8 44.6 %all_gather.28 = s32[4096,8]{0,1:T(8,128)S(1)} all-gather(s32[128,8]{0,1:T(8,128)} %param.12), channel_id=1, replica_groups=mesh['row'=8,'col'=32] {'col'}, dimensions={0}, use_global_device_ids=true | all-gather | bytes 135168 | tf_op jit(solution)/shard_map/all_gather | solution.py:123
  173.5 37.9 %all_gather.25 = bf16[1024,128]{1,0:T(8,128)(2,1)S(1)} all-gather(bf16[128,128]{1,0:T(8,128)(2,1)} %param.10), channel_id=1, replica_groups=mesh['row'=8,'col'=32] {'row'}, dimensions={0}, use_global_device_ids=true | all-gather | bytes 294912 | tf_op jit(solution)/shard_map/all_gather | solution.py:133
  214.6 266.5 %while.32 = (s32[]{:T(128)}, f32[32,128,8]{1,2,0:T(8,128)S(1)}, f32[8,128,8]{1,2,0:T(8,128)S(1)}, s32[]{:T(128)}, s32[256]{0:T(256)}, /*index=5*/bf16[32,128,128...) while((s32[]{:T(128)}, f32[32,128,8]{1,2,0:T(8,128)S(1)}, ...), condition=%wide.region_9.11_spmd.clone.clone, body=%wide.region_4.10_spmd.clone.clone.sunk | while | flops 213377504 | bytes 27038416 | solution.py:102
  224.0 9.3 fusion.174
  253.6 9.3 fusion.174
  283.2 9.3 fusion.174
  312.8 9.3 fusion.174
  342.3 9.3 fusion.174
  371.9 9.3 fusion.174
  401.5 9.3 fusion.174
  431.1 9.3 fusion.174
  460.7 9.3 fusion.174
  484.7 39.5 %all-reduce.1 = f32[8,128,8]{1,2,0:T(8,128)S(1)} all-reduce(f32[8,128,8]{1,2,0:T(8,128)S(1)} %get-tuple-element.391), channel_id=3, replica_groups=mesh['row'=8,'col'=32] {'row'}, use_global_device_ids=true, to_apply=%region_11.13.clone | all-reduce | flops 8192 | bytes 65536
  524.3 203.3 %all-reduce.8.cloned.1.call-done = f32[32,128,8]{1,2,0:T(8,128)} async-done(((f32[32,128,8]{1,2,0:T(8,128)}), f32[32,128,8]{1,2,0:T(8,128)}) %all-reduce.8.cloned.1.call-update) | async-done | bytes 131088
  730.1 39.7 %all_gather.31 = bf16[4096,8]{0,1:T(8,128)(2,1)S(1)} all-gather(bf16[128,8]{0,1:T(8,128)(2,1)S(1)} %get-tuple-element.780), channel_id=1, replica_groups=mesh['row'=8,'col'=32] {'col'}, dimensions={0}, use_global_device_ids=true | all-gather | bytes 67584 | tf_op jit(solution)/shard_map/all_gather | solution.py:164
  769.7 35.1 %all_gather.30 = bf16[1024,8]{0,1:T(8,128)(2,1)S(1)} all-gather(bf16[128,8]{0,1:T(8,128)(2,1)S(1)} %get-tuple-element.780), channel_id=1, replica_groups=mesh['row'=8,'col'=32] {'row'}, dimensions={0}, use_global_device_ids=true | all-gather | bytes 18432 | tf_op jit(solution)/shard_map/all_gather | solution.py:167
  804.8 144.6 %while.33 = (s32[]{:T(128)}, f32[32,128,8]{1,2,0:T(8,128)S(1)}, f32[8,128,8]{1,2,0:T(8,128)S(1)}, s32[]{:T(128)}, s32[256]{0:T(256)}, /*index=5*/bf16[32,128,128...) while((s32[]{:T(128)}, f32[32,128,8]{1,2,0:T(8,128)S(1)}, ...), condition=%wide.region_19.21_spmd.clone.clone, body=%wide.region_14.20_spmd.clone.clone.sunk | while | flops 205513184 | bytes 14005563 | solution.py:102
  950.7 45.4 %all-reduce.3 = f32[8,128,8]{1,2,0:T(8,128)S(1)} all-reduce(f32[8,128,8]{1,2,0:T(8,128)S(1)} %get-tuple-element.393), channel_id=5, replica_groups=mesh['row'=8,'col'=32] {'row'}, use_global_device_ids=true, to_apply=%region_21.23.clone | all-reduce | flops 8192 | bytes 65536
  996.1 204.5 %all-reduce.10.cloned.1.call-done = f32[32,128,8]{1,2,0:T(8,128)} async-done(((f32[32,128,8]{1,2,0:T(8,128)}), f32[32,128,8]{1,2,0:T(8,128)}) %all-reduce.10.cloned.1.call-update) | async-done | bytes 131088
  1202.7 77.4 %all-reduce.4 = (f32[8]{0:T(128)S(1)}, f32[8]{0:T(128)S(1)}, f32[8]{0:T(128)S(1)}) all-reduce(f32[8]{0:T(128)S(1)} %get-tuple-element.680, f32[8]{0:T(128)S(1)} %get-tuple-element.679, f32[8]{0:T(128)S(1)} %get-tuple-element.678), channel_id=1, replica_groups=mesh['row'=8,'col'=32] {'row','col'}, use_global_device_ids=true, to_apply=%region_13.15 | all-reduce | flops 24 | bytes 192 | tf_op jit(solution)/shard_map/psum | solution.py:178
  (920 shorter events, 343.2 us)
Async XLA Ops:
  7.2 205.5 %all-gather.4.cloned.1.call-start = ((), (), s32[]{:S(2)}) async-start(), calls=%async_computation | async-start | bytes 1081344 | tf_op jit(solution)/shard_map/all_gather | solution.py:137
  7.9 719.6 %all-reduce.8.cloned.1.call-start = ((), (), s32[]{:S(2)}) async-start(), calls=%async_computation.1 | async-start | bytes 262144
  224.0 10.3 copy-start.6
  224.0 10.4 copy-start.8
  253.6 10.3 copy-start.6
  253.6 10.4 copy-start.8
  283.2 10.3 copy-start.6
  283.2 10.4 copy-start.8
  312.8 10.3 copy-start.6
  312.8 10.4 copy-start.8
  342.3 10.3 copy-start.6
  342.3 10.4 copy-start.8
  358.6 3.0 copy-start.3
  371.9 10.3 copy-start.6
  371.9 10.4 copy-start.8
  401.5 10.3 copy-start.6
  401.5 10.4 copy-start.8
  417.7 3.0 copy-start.3
  431.1 10.3 copy-start.6
  431.1 10.4 copy-start.8
  460.7 10.3 copy-start.6
  460.7 10.4 copy-start.8
  476.9 3.0 copy-start.3
  481.7 718.9 %all-reduce.10.cloned.1.call-start = ((), (), s32[]{:S(2)}) async-start(), calls=%async_computation.2 | async-start | bytes 262144
  (62 other events, 84.8 us)
Sparse Core Ops, SparseCore 0:
  9.9 63.0 all-gather.3
  481.9 245.6 all-reduce.7
  950.2 250.3 all-reduce.9
where the time goes:
time: 1290 us
  blocking collectives  432 us (33%)
  waiting for transfers between devices  409 us (32%)
  other arithmetic  221 us (17%)
  local copies, waits for them, and re-layouts  183 us (14%)
  matrix products  25.4 us (2%)
  between operations  14.6 us (1%)
    unnamed x5, waiting for transfers between devices  408 us
    convert_element_type x56, other arithmetic, action_features(): jnp.where(levels == 0, constant_term, wave_terms).astype(jnp.bfloat16)  130 us
    unnamed x2, blocking collectives  84.9 us
    psum x1, blocking collectives, on_device(): lax.psum((jnp.sum(right_side * right_side, axis=0), jnp.sum(right_side *...  77.4 us
    all_gather x1, blocking collectives, on_device(): lax.all_gather(logged_actions, 'col', axis=0, tiled=True)  46.1 us
    all_gather x1, blocking collectives, on_device(): lax.all_gather(policy_actions, 'col', axis=0, tiled=True)  44.6 us
    all_gather x1, blocking collectives, on_device(): lax.all_gather(right_low, 'col', axis=0, tiled=True)  39.7 us
    all_gather x1, blocking collectives, on_device(): lax.all_gather(contexts, 'row', axis=0, tiled=True)  37.9 us
  transfers between devices with their start and end apart: 3, of which 2 were waited for; matrix products, arithmetic and copies ran while one was open for 1% of the time, Pallas kernels for 0%

commit v1 on v0

--- a/solution.py
+++ b/solution.py
@@ -176,12 +176,15 @@
     second_left, second_right = sweep(left_second, right_second)
     image = reduce_terms(second_left, second_right) + ridge * right_side
     norm_sums, curvature, reward_sums = lax.psum(
-        (
-            jnp.sum(right_side * right_side, axis=0),
-            jnp.sum(right_side * image, axis=0),
-            jnp.sum(rewards[:, None] * right_side, axis=0),
+        lax.psum(
+            (
+                jnp.sum(right_side * right_side, axis=0),
+                jnp.sum(right_side * image, axis=0),
+                jnp.sum(rewards[:, None] * right_side, axis=0),
+            ),
+            "row",
         ),
-        ("row", "col"),
+        "col",
     )
     alpha = norm_sums / curvature
     weights = alpha[None, :] * right_side

time: 1290 us -> 1310 us (1.016)
  blocking collectives: 432 us -> 455 us
    psum x0 -> x1, blocking collectives: none -> 74.2 us  [on_device(): lax.psum(lax.psum((jnp.sum(right_side * right_side, axis=0), jnp.sum(righ...]
    psum x1, blocking collectives: 77.4 us -> 26 us  [on_device(): lax.psum((jnp.sum(right_side * right_side, axis=0), jnp.sum(right_side *...]
where the time goes in v1:
time: 1310 us
  blocking collectives  455 us (35%)
  waiting for transfers between devices  408 us (31%)
  other arithmetic  221 us (17%)
  local copies, waits for them, and re-layouts  183 us (14%)
  matrix products  25.5 us (2%)
  between operations  14.6 us (1%)
    unnamed x5, waiting for transfers between devices  408 us
    convert_element_type x56, other arithmetic, action_features(): jnp.where(levels == 0, constant_term, wave_terms).astype(jnp.bfloat16)  130 us
    unnamed x2, blocking collectives  84.9 us
    psum x1, blocking collectives, on_device(): lax.psum(lax.psum((jnp.sum(right_side * right_side, axis=0), jnp.sum(righ...  74.2 us
    all_gather x1, blocking collectives, on_device(): lax.all_gather(logged_actions, 'col', axis=0, tiled=True)  46.1 us
    all_gather x1, blocking collectives, on_device(): lax.all_gather(policy_actions, 'col', axis=0, tiled=True)  44.6 us
    all_gather x1, blocking collectives, on_device(): lax.all_gather(right_low, 'col', axis=0, tiled=True)  39.7 us
    all_gather x1, blocking collectives, on_device(): lax.all_gather(contexts, 'row', axis=0, tiled=True)  37.9 us
  transfers between devices with their start and end apart: 3, of which 2 were waited for; matrix products, arithmetic and copies ran while one was open for 1% of the time, Pallas kernels for 0%

profile of v1, /device:TPU:1, one launch (start us, length us, event | category | flops | bytes accessed | tf_op | source)
XLA Modules:
  0.0 1311.6 jit_solution(13944894183374665811)
XLA Ops:
  14.8 29.4 %all-gather.1 = s32[8,1,128]{2,1,0:T(1,128)S(1)} all-gather(s32[1,1,128]{2,1,0:T(1,128)} %bitcast.113), channel_id=1, replica_groups=mesh['row'=8,'col'=32] {'row'}, dimensions={0}, use_global_device_ids=true | all-gather | bytes 4608 | tf_op jit(solution)/shard_map/all_gather | solution.py:126
  44.2 46.1 %all-gather = s32[32,1,128]{2,1,0:T(1,128)S(1)} all-gather(s32[1,1,128]{2,1,0:T(1,128)} %bitcast.114), channel_id=1, replica_groups=mesh['row'=8,'col'=32] {'col'}, dimensions={0}, use_global_device_ids=true | all-gather | bytes 16896 | tf_op jit(solution)/shard_map/all_gather | solution.py:122
  90.3 37.4 %all_gather.26 = s32[1024,8]{0,1:T(8,128)S(1)} all-gather(s32[128,8]{0,1:T(8,128)} %param.12), channel_id=1, replica_groups=mesh['row'=8,'col'=32] {'row'}, dimensions={0}, use_global_device_ids=true | all-gather | bytes 36864 | tf_op jit(solution)/shard_map/all_gather | solution.py:127
  127.8 44.6 %all_gather.28 = s32[4096,8]{0,1:T(8,128)S(1)} all-gather(s32[128,8]{0,1:T(8,128)} %param.12), channel_id=1, replica_groups=mesh['row'=8,'col'=32] {'col'}, dimensions={0}, use_global_device_ids=true | all-gather | bytes 135168 | tf_op jit(solution)/shard_map/all_gather | solution.py:123
  173.5 37.9 %all_gather.25 = bf16[1024,128]{1,0:T(8,128)(2,1)S(1)} all-gather(bf16[128,128]{1,0:T(8,128)(2,1)} %param.10), channel_id=1, replica_groups=mesh['row'=8,'col'=32] {'row'}, dimensions={0}, use_global_device_ids=true | all-gather | bytes 294912 | tf_op jit(solution)/shard_map/all_gather | solution.py:133
  214.6 266.5 %while.32 = (s32[]{:T(128)}, f32[32,128,8]{1,2,0:T(8,128)S(1)}, f32[8,128,8]{1,2,0:T(8,128)S(1)}, s32[]{:T(128)}, s32[256]{0:T(256)}, /*index=5*/bf16[32,128,128...) while((s32[]{:T(128)}, f32[32,128,8]{1,2,0:T(8,128)S(1)}, ...), condition=%wide.region_9.11_spmd.clone.clone, body=%wide.region_4.10_spmd.clone.clone.sunk | while | flops 213377504 | bytes 27038416 | solution.py:102
  224.0 9.3 fusion.174
  253.6 9.3 fusion.174
  283.2 9.3 fusion.174
  312.8 9.3 fusion.174
  342.4 9.3 fusion.174
  371.9 9.3 fusion.174
  401.5 9.3 fusion.174
  431.1 9.3 fusion.174
  460.7 9.3 fusion.174
  484.8 39.5 %all-reduce.1 = f32[8,128,8]{1,2,0:T(8,128)S(1)} all-reduce(f32[8,128,8]{1,2,0:T(8,128)S(1)} %get-tuple-element.391), channel_id=3, replica_groups=mesh['row'=8,'col'=32] {'row'}, use_global_device_ids=true, to_apply=%region_11.13.clone | all-reduce | flops 8192 | bytes 65536
  524.3 203.0 %all-reduce.9.cloned.1.call-done = f32[32,128,8]{1,2,0:T(8,128)} async-done(((f32[32,128,8]{1,2,0:T(8,128)}), f32[32,128,8]{1,2,0:T(8,128)}) %all-reduce.9.cloned.1.call-update) | async-done | bytes 131088
  729.8 39.7 %all_gather.31 = bf16[4096,8]{0,1:T(8,128)(2,1)S(1)} all-gather(bf16[128,8]{0,1:T(8,128)(2,1)S(1)} %get-tuple-element.783), channel_id=1, replica_groups=mesh['row'=8,'col'=32] {'col'}, dimensions={0}, use_global_device_ids=true | all-gather | bytes 67584 | tf_op jit(solution)/shard_map/all_gather | solution.py:164
  769.4 35.1 %all_gather.30 = bf16[1024,8]{0,1:T(8,128)(2,1)S(1)} all-gather(bf16[128,8]{0,1:T(8,128)(2,1)S(1)} %get-tuple-element.783), channel_id=1, replica_groups=mesh['row'=8,'col'=32] {'row'}, dimensions={0}, use_global_device_ids=true | all-gather | bytes 18432 | tf_op jit(solution)/shard_map/all_gather | solution.py:167
  804.5 144.3 %while.33 = (s32[]{:T(128)}, f32[32,128,8]{1,2,0:T(8,128)S(1)}, f32[8,128,8]{1,2,0:T(8,128)S(1)}, s32[]{:T(128)}, s32[256]{0:T(256)}, /*index=5*/bf16[32,128,128...) while((s32[]{:T(128)}, f32[32,128,8]{1,2,0:T(8,128)S(1)}, ...), condition=%wide.region_20.22_spmd.clone.clone, body=%wide.region_15.21_spmd.clone.clone.sunk | while | flops 205513184 | bytes 14005563 | solution.py:102
  950.2 45.4 %all-reduce.3 = f32[8,128,8]{1,2,0:T(8,128)S(1)} all-reduce(f32[8,128,8]{1,2,0:T(8,128)S(1)} %get-tuple-element.393), channel_id=5, replica_groups=mesh['row'=8,'col'=32] {'row'}, use_global_device_ids=true, to_apply=%region_22.24.clone | all-reduce | flops 8192 | bytes 65536
  995.5 204.0 %all-reduce.11.cloned.1.call-done = f32[32,128,8]{1,2,0:T(8,128)} async-done(((f32[32,128,8]{1,2,0:T(8,128)}), f32[32,128,8]{1,2,0:T(8,128)}) %all-reduce.11.cloned.1.call-update) | async-done | bytes 131088
  1201.7 26.0 %all-reduce.5 = (f32[8]{0:T(128)S(1)}, f32[8]{0:T(128)S(1)}, f32[8]{0:T(128)S(1)}) all-reduce(f32[8]{0:T(128)S(1)} %get-tuple-element.680, f32[8]{0:T(128)S(1)} %get-tuple-element.679, f32[8]{0:T(128)S(1)} %get-tuple-element.678), channel_id=1, replica_groups=mesh['row'=8,'col'=32] {'row'}, use_global_device_ids=true, to_apply=%region_13.15 | all-reduce | flops 24 | bytes 192 | tf_op jit(solution)/shard_map/psum | solution.py:179
  1227.7 74.2 %all-reduce.4 = (f32[8]{0:T(128)S(1)}, f32[8]{0:T(128)S(1)}, f32[8]{0:T(128)S(1)}) all-reduce(f32[8]{0:T(128)S(1)} %get-tuple-element.774, f32[8]{0:T(128)S(1)} %get-tuple-element.775, f32[8]{0:T(128)S(1)} %get-tuple-element.776), channel_id=1, replica_groups=mesh['row'=8,'col'=32] {'col'}, use_global_device_ids=true, to_apply=%region_14.16 | all-reduce | flops 24 | bytes 192 | tf_op jit(solution)/shard_map/psum | solution.py:178
  (921 shorter events, 346.1 us)
Async XLA Ops:
  7.2 205.5 %all-gather.4.cloned.1.call-start = ((), (), s32[]{:S(2)}) async-start(), calls=%async_computation | async-start | bytes 1081344 | tf_op jit(solution)/shard_map/all_gather | solution.py:137
  7.9 719.4 %all-reduce.9.cloned.1.call-start = ((), (), s32[]{:S(2)}) async-start(), calls=%async_computation.1 | async-start | bytes 262144
  224.0 10.3 copy-start.6
  224.0 10.4 copy-start.8
  253.6 10.3 copy-start.6
  253.6 10.4 copy-start.8
  269.8 3.0 copy-start.3
  283.2 10.3 copy-start.6
  283.2 10.4 copy-start.8
  312.8 10.3 copy-start.6
  312.8 10.4 copy-start.8
  342.3 10.4 copy-start.6
  342.4 10.4 copy-start.8
  358.6 3.0 copy-start.3
  371.9 10.3 copy-start.6
  371.9 10.4 copy-start.8
  388.2 3.0 copy-start.3
  401.5 10.3 copy-start.6
  401.5 10.4 copy-start.8
  431.1 10.3 copy-start.6
  431.1 10.4 copy-start.8
  460.7 10.4 copy-start.6
  460.7 10.4 copy-start.8
  481.8 717.8 %all-reduce.11.cloned.1.call-start = ((), (), s32[]{:S(2)}) async-start(), calls=%async_computation.2 | async-start | bytes 262144
  (62 other events, 84.3 us)
Sparse Core Ops, SparseCore 0:
  9.9 63.0 all-gather.3
  481.9 245.3 all-reduce.8
  949.6 249.9 all-reduce.10
